TPU v7x, 32 devices: a whole 2x2x4 slice. The times are simulated.
32 devices in a mesh: lat: 4 (over y, core), lon: 4 (over z), mesh: 2 (over x).
Axes of the slice: x: 2, y: 2, z: 4, core: 2. Of those that a mesh axis runs over, the one named last changes fastest.
Arguments:
- grid_latent: bfloat16 [32768, 512], P(('lat', 'lon', 'mesh')), may hold values from -6 to 6
- target: bfloat16 [32768, 84], P(('lat', 'lon', 'mesh')), may hold values from -6 to 6
- area: float32 [32768], P(('lat', 'lon', 'mesh')), may hold values from 0.05 to 1
- mesh_latent: bfloat16 [10240, 512], P(('lat', 'lon', 'mesh')), may hold values from -6 to 6
- node_gain: float32 [512], replicated, may hold values from 0.1 to 1.9
- w_enc: bfloat16 [512, 512], replicated, may hold values from -0.25 to 0.25
- w_up: bfloat16 [512, 512], replicated, may hold values from -0.25 to 0.25
- w_down: bfloat16 [512, 512], replicated, may hold values from -0.25 to 0.25
- w_msg: bfloat16 [512, 512], replicated, may hold values from -0.25 to 0.25
- w_dec: bfloat16 [512, 512], replicated, may hold values from -0.25 to 0.25
- w_out: bfloat16 [512, 84], replicated, may hold values from -0.25 to 0.25
- enc_cell: int32 [32, 3, 3, 2, 85], P(('lat', 'lon', 'mesh')), may hold values from 0 to 1023
- enc_live: int32 [32, 3, 3, 2], P(('lat', 'lon', 'mesh')), may hold values from 1 to 85, as said below
- enc_weight: float32 [32, 3, 3, 2, 85], P(('lat', 'lon', 'mesh')), may hold values from 0.2 to 1
- enc_node: int32 [32, 3, 3, 2, 85], P(('lat', 'lon', 'mesh')), may hold values from 0 to 319
- dec_node: int32 [32, 3, 3, 2, 128], P(('lat', 'lon', 'mesh')), may hold values from 0 to 319
- dec_cell: int32 [32, 3, 3, 2, 128], P(('lat', 'lon', 'mesh')), may hold values from 0 to 1023
- dec_weight: float32 [32, 3, 3, 2, 128], P(('lat', 'lon', 'mesh')), may hold values from 0.2 to 1
Outputs:
- grid_grad: float32 [32768, 512], P(('lat', 'lon', 'mesh'))
- grad_enc: float32 [512, 512], P(('lat', 'lon', 'mesh'))
- grad_up: float32 [512, 512], P(('lat', 'lon', 'mesh'))
- grad_down: float32 [512, 512], P(('lat', 'lon', 'mesh'))
- grad_msg: float32 [512, 512], P(('lat', 'lon', 'mesh'))
- grad_dec: float32 [512, 512], P(('lat', 'lon', 'mesh'))
- grad_out: float32 [512, 84], P(('lat', 'lon', 'mesh'))
Inputs may be any that keep to these rules, and one draw needn't show every extreme that they name: Slots 0 to enc_live - 1 of a bucket are edges, the others padding; in every draw some mesh owner receives 85 live slots in every bucket addressed to it. `enc_cell`: local cell indices. `enc_node`: local node indices. `dec_node`: local node indices. `dec_cell`: local cell indices.
All inputs are finite; a program needn't handle non-finite values.
Results may differ from a plain program's by a relative error of at most 0.0085.
Values may be sent and summed in bfloat16 or wider, within the bound.
No kernel may reach another device: no remote copies, remote signals or barrier semaphores. Data moves between devices by JAX's collectives and lax.ppermute only.
A program may use at most 128 MiB of HBM per device.

v0:
```python
import jax
import jax.numpy as jnp
from jax import lax
from jax.sharding import PartitionSpec as P


def extended_2(cells, sides, width):
    for axis, dim in sides:
        count = lax.axis_size(axis)
        head = lax.slice_in_dim(cells, 0, width, axis=dim)
        tail = lax.slice_in_dim(cells, cells.shape[dim] - width, cells.shape[dim], axis=dim)
        cells = jnp.concatenate(
            [
                lax.ppermute(tail, axis, [(i, (i + 1) % count) for i in range(count)]),
                cells,
                lax.ppermute(head, axis, [((i + 1) % count, i) for i in range(count)]),
            ],
            axis=dim,
        )
    return cells


def matmul(left, right):
    return jnp.dot(left, right, preferred_element_type=jnp.float32)


def contract(left, right):
    return lax.dot_general(
        left, right, (((0,), (0,)), ((), ())), preferred_element_type=jnp.float32
    )


def silu_slope(argument):
    sigmoid_value = jax.nn.sigmoid(argument)
    return sigmoid_value * (1.0 + argument * (1.0 - sigmoid_value))


def node_forward(node_state, node_gain, w_up, w_down):
    inv_rms = lax.rsqrt(jnp.mean(node_state * node_state, axis=-1, keepdims=True) + 1e-05)
    normed = (node_state * inv_rms * node_gain).astype(jnp.bfloat16)
    activation = matmul(normed, w_up)
    hidden = jax.nn.silu(activation).astype(jnp.bfloat16)
    updated = node_state + matmul(hidden, w_down)
    return (updated, inv_rms, normed, activation, hidden)


def node_backward(
    back_node, node_state, node_gain, w_up, w_down, inv_rms, normed, activation, hidden
):
    back_node_half = back_node.astype(jnp.bfloat16)
    grad_down = contract(hidden, back_node_half)
    back_hidden = matmul(back_node_half, w_down.T)
    back_act = (back_hidden * silu_slope(activation)).astype(jnp.bfloat16)
    grad_up = contract(normed, back_act)
    back_norm = matmul(back_act, w_up.T) * node_gain
    mean_term = jnp.mean(node_state * back_norm, axis=-1, keepdims=True)
    back_state = back_node + inv_rms * back_norm - node_state * inv_rms**3 * mean_term
    return (back_state, grad_up, grad_down)


def route_enc(bucket):
    crossed = lax.all_to_all(bucket, "mesh", split_axis=2, concat_axis=2, tiled=True)
    extended = extended_2(crossed, (("lat", 0), ("lon", 1)), 1)
    result = extended[::-2, ::-2]
    return result


def route_dec(bucket):
    crossed = lax.all_to_all(bucket, "mesh", split_axis=2, concat_axis=2, tiled=True)
    extended = extended_2(crossed, (("lat", 0), ("lon", 1)), 1)
    result = extended[::-2, ::-2]
    return result


def on_device(
    grid_latent,
    target,
    area,
    mesh_latent,
    node_gain,
    w_enc,
    w_up,
    w_down,
    w_msg,
    w_dec,
    w_out,
    enc_cell,
    enc_live,
    enc_weight,
    enc_node,
    dec_node,
    dec_cell,
    dec_weight,
):
    cell_rows = grid_latent.shape[0]
    node_rows = mesh_latent.shape[0]
    features = grid_latent.shape[1]
    send_cells = enc_cell[0]
    offsets = jnp.arange(3, dtype=jnp.int32) - 1
    lat_here = lax.axis_index("lat")
    lat_count = lax.axis_size("lat")
    reach_up = lat_here + offsets
    send_ok = (reach_up >= 0) & (reach_up < lat_count)
    reach_down = lat_here - offsets
    recv_ok = (reach_down >= 0) & (reach_down < lat_count)
    slot_index = jnp.arange(send_cells.shape[-1], dtype=jnp.int32)
    edge_scale = jnp.where(
        (slot_index < enc_live[0][..., None]) & send_ok[:, None, None, None],
        enc_weight[0],
        jnp.float32(0.0),
    )
    dec_scale = jnp.where(recv_ok[:, None, None, None], dec_weight[0], jnp.float32(0.0))
    projected = matmul(grid_latent, w_enc).astype(jnp.bfloat16)
    outgoing = (edge_scale[..., None] * projected[send_cells].astype(jnp.float32)).astype(
        jnp.bfloat16
    )
    landed = route_enc(outgoing)
    aggregate = jax.ops.segment_sum(
        landed.reshape(-1, features).astype(jnp.float32),
        enc_node[0].reshape(-1),
        num_segments=node_rows,
    )
    node_state = mesh_latent.astype(jnp.float32) + aggregate
    updated, inv_rms, normed, activation, hidden = node_forward(node_state, node_gain, w_up, w_down)
    node_half = updated.astype(jnp.bfloat16)
    leaving = node_half[dec_node[0]]
    pulled = route_dec(leaving)
    row_block = pulled.reshape(-1, features)
    preact = matmul(row_block, w_msg)
    edge_weight = dec_scale.reshape(-1)[:, None]
    cell_ids = dec_cell[0].reshape(-1)
    weighted = edge_weight * jax.nn.silu(preact)
    gathered = jax.ops.segment_sum(weighted, cell_ids, num_segments=cell_rows).astype(jnp.bfloat16)
    blended = grid_latent.astype(jnp.float32) + matmul(gathered, w_dec)
    blended_half = blended.astype(jnp.bfloat16)
    output = matmul(blended_half, w_out)
    residual = (area[:, None] * (output - target.astype(jnp.float32))).astype(jnp.bfloat16)
    grad_out = contract(blended_half, residual) / cell_rows
    back_blend = matmul(residual, w_out.T)
    back_half = back_blend.astype(jnp.bfloat16)
    grad_dec = contract(gathered, back_half) / cell_rows
    back_gather = matmul(back_half, w_dec.T).astype(jnp.bfloat16)
    back_message = edge_weight * back_gather[cell_ids].astype(jnp.float32)
    back_preact = (back_message * silu_slope(preact)).astype(jnp.bfloat16)
    grad_msg = contract(row_block, back_preact) / cell_rows
    back_pulled = matmul(back_preact, w_msg.T).astype(jnp.bfloat16).reshape(pulled.shape)
    returned = route_dec(back_pulled[::-1, ::-1])[::-1, ::-1]
    back_node = jax.ops.segment_sum(
        returned.reshape(-1, features).astype(jnp.float32),
        dec_node[0].reshape(-1),
        num_segments=node_rows,
    )
    back_state, grad_up, grad_down = node_backward(
        back_node, node_state, node_gain, w_up, w_down, inv_rms, normed, activation, hidden
    )
    back_state_half = back_state.astype(jnp.bfloat16)
    toward = back_state_half[enc_node[0]]
    came_back = route_enc(toward[::-1, ::-1])[::-1, ::-1]
    weighted_back = (edge_scale[..., None] * came_back.astype(jnp.float32)).reshape(-1, features)
    back_proj = jax.ops.segment_sum(
        weighted_back, send_cells.reshape(-1), num_segments=cell_rows
    ).astype(jnp.bfloat16)
    grad_enc = contract(grid_latent, back_proj) / cell_rows
    grid_grad = back_blend + matmul(back_proj, w_enc.T)
    partials = (grad_enc, grad_up / cell_rows, grad_down / cell_rows, grad_msg, grad_dec, grad_out)
    totals = lax.psum(
        (partials[0], partials[1], partials[2], partials[3], partials[4], partials[5]),
        ("lat", "lon", "mesh"),
    )
    row_share = features // lax.axis_size(("lat", "lon", "mesh"))
    row_start = lax.axis_index(("lat", "lon", "mesh")) * row_share
    shares = tuple((lax.dynamic_slice_in_dim(total, row_start, row_share, 0) for total in totals))
    return (grid_grad,) + tuple(shares)


def solution(mesh):
    placed = (
        P(("lat", "lon", "mesh"), None),
        P(("lat", "lon", "mesh"), None),
        P(("lat", "lon", "mesh")),
        P(("lat", "lon", "mesh"), None),
        P(),
        P(),
        P(),
        P(),
        P(),
        P(),
        P(),
        P(("lat", "lon", "mesh"), None, None, None, None),
        P(("lat", "lon", "mesh"), None, None, None),
        P(("lat", "lon", "mesh"), None, None, None, None),
        P(("lat", "lon", "mesh"), None, None, None, None),
        P(("lat", "lon", "mesh"), None, None, None, None),
        P(("lat", "lon", "mesh"), None, None, None, None),
        P(("lat", "lon", "mesh"), None, None, None, None),
    )
    return jax.shard_map(
        on_device,
        mesh=mesh,
        in_specs=placed,
        out_specs=(
            P(("lat", "lon", "mesh"), None),
            P(("lat", "lon", "mesh"), None),
            P(("lat", "lon", "mesh"), None),
            P(("lat", "lon", "mesh"), None),
            P(("lat", "lon", "mesh"), None),
            P(("lat", "lon", "mesh"), None),
            P(("lat", "lon", "mesh"), None),
        ),
        check_vma=False,
    )
```

profile of v0, /device:TPU:0, one launch (start us, length us, event | category | flops | bytes accessed | tf_op | source)
XLA Modules:
  0.0 727.9 jit_solution(15352589680667660315)
XLA Ops:
  12.3 4.8 gather_fusion
  22.3 23.8 %all_to_all.20 = bf16[3,3,2,85,512]{4,3,1,0,2:T(8,128)(2,1)S(1)} all-to-all(bf16[3,3,2,85,512]{4,3,1,0,2:T(8,128)(2,1)S(1)} %copy.55), channel_id=1, replica_groups=mesh['lat'=4,'lon'=4,'mesh'=2] {'mesh'}, dimensions={2} | all-to-all | bytes 3133440 | tf_op jit(solution)/shard_map/all_to_all | solution.py:62
  48.8 9.5 %collective-permute-done = bf16[1,3,2,85,512]{4,2,3,1,0:T(2,128)(2,1)S(1)} collective-permute-done((bf16[1,3,2,85,512]{4,2,3,1,0:T(2,128)(2,1)S(1)}, bf16[1,3,2,85,512]{4,2,3,1,0:T(2,128)(2,1)S(1)}, u32[]{:S(2)}, u32[]{:S(2)}) %collective-permute-start) | collective-permute-done | bytes 522272 | tf_op jit(solution)/shard_map/ppermute | solution.py:14
  61.0 3.7 collective-permute-start.3
  67.2 17.3 %collective-permute-done.3 = bf16[5,1,2,85,512]{4,2,3,1,0:T(2,128)(2,1)S(1)} collective-permute-done((bf16[5,1,2,85,512]{4,2,3,1,0:T(2,128)(2,1)S(1)}, bf16[5,1,2,85,512]{4,2,3,1,0:T(2,128)(2,1)S(1)}, u32[]{:S(2)}, u32[]{:S(2)}) %collective-permute-start.3) | collective-permute-done | bytes 870432 | tf_op jit(solution)/shard_map/ppermute | solution.py:16
  84.6 19.3 %collective-permute-done.2 = bf16[5,1,2,85,512]{4,2,3,1,0:T(2,128)(2,1)} collective-permute-done((bf16[5,1,2,85,512]{4,2,3,1,0:T(2,128)(2,1)}, bf16[5,1,2,85,512]{4,2,3,1,0:T(2,128)(2,1)}, u32[]{:S(2)}, u32[]{:S(2)}) %collective-permute-start.2) | collective-permute-done | bytes 870432 | tf_op jit(solution)/shard_map/ppermute | solution.py:14
  108.4 3.6 reshape.237
  112.0 10.6 %scatter_fusion = f32[320,512]{1,0:T(8,128)S(1)} fusion(f32[320,512]{1,0:T(8,128)S(1)} %convert_element_type.79, s32[1530]{0:T(1024)S(1)} %reshape.235, f32[1530,512]{1,0:T(8,128)} %reshape.237), kind=kCustom, calls=%fused_computation.4 | custom fusion | flops 783360 | bytes 9406440 | tf_op jit(solution)/shard_map/scatter-add | solution.py:118
  125.0 7.5 %gather_fusion.1 = bf16[2304,512]{1,0:T(8,128)(2,1)} fusion(bf16[320,512]{1,0:T(8,128)(2,1)S(1)} %fusion.6, s32[3072]{0:T(1024)S(1)} %get-tuple-element.62), kind=kCustom, calls=%fused_computation.1 | custom fusion | bytes 4727808 | tf_op jit(solution)/shard_map/gather | solution.py:126
  134.3 30.6 %all_to_all.21 = bf16[3,3,2,128,512]{4,3,1,0,2:T(8,128)(2,1)S(1)} all-to-all(bf16[3,3,2,128,512]{4,3,1,0,2:T(8,128)(2,1)S(1)} %copy.65), channel_id=1, replica_groups=mesh['lat'=4,'lon'=4,'mesh'=2] {'mesh'}, dimensions={2} | all-to-all | bytes 4718592 | tf_op jit(solution)/shard_map/all_to_all | solution.py:69
  167.6 14.9 %collective-permute-done.4 = bf16[1,3,2,128,512]{4,3,2,1,0:T(8,128)(2,1)S(1)} collective-permute-done((bf16[1,3,2,128,512]{4,3,2,1,0:T(8,128)(2,1)S(1)}, bf16[1,3,2,128,512]{4,3,2,1,0:T(8,128)(2,1)S(1)}, u32[]{:S(2)}, u32[]{:S(2)}) %collective-permute-start.4) | collective-permute-done | bytes 786464 | tf_op jit(solution)/shard_map/ppermute | solution.py:14
  192.5 29.1 %collective-permute-done.6 = bf16[5,1,2,128,512]{4,3,2,1,0:T(8,128)(2,1)S(1)} collective-permute-done((bf16[5,1,2,128,512]{4,3,2,1,0:T(8,128)(2,1)}, bf16[5,1,2,128,512]{4,3,2,1,0:T(8,128)(2,1)S(1)}, u32[]{:S(2)}, u32[]{:S(2)}) %collective-permute-start.6) | collective-permute-done | bytes 1310752 | tf_op jit(solution)/shard_map/ppermute | solution.py:14
  221.6 27.4 %collective-permute-done.7 = bf16[5,1,2,128,512]{4,3,2,1,0:T(8,128)(2,1)} collective-permute-done((bf16[5,1,2,128,512]{4,3,2,1,0:T(8,128)(2,1)}, bf16[5,1,2,128,512]{4,3,2,1,0:T(8,128)(2,1)}, u32[]{:S(2)}, u32[]{:S(2)}) %collective-permute-start.7) | collective-permute-done | bytes 1310752 | tf_op jit(solution)/shard_map/ppermute | solution.py:16
  257.2 3.5 fusion.33
  260.7 22.0 %scatter_custom_fusion.1 = f32[1024,512]{1,0:T(8,128)S(1)} fusion(s32[2304]{0:T(1024)} %reshape.243, f32[2304,512]{1,0:T(8,128)} %fusion.33, f32[]{:T(128)} %constant.24.clone.1, f32[2304]{0:T(1024)S(1)} %broadcast_select_fusion, f32[]{:T(128)} %constant.16.clone.1), kind=kCustom, calls=%fused_computation.11 | custom fusion | flops 7077888 | bytes 6825984 | tf_op jit(solution)/shard_map/scatter-add | solution.py:133
  290.3 7.5 %gather_fusion.2 = bf16[2304,512]{1,0:T(8,128)(2,1)} fusion(bf16[1024,512]{1,0:T(8,128)(2,1)S(1)} %convolution_convert_fusion.1, s32[3072]{0:T(1024)S(1)} %copy-done.31), kind=kCustom, calls=%fused_computation.2 | custom fusion | bytes 4727808 | tf_op jit(solution)/shard_map/gather | solution.py:143
  297.9 4.1 multiply_convert_fusion
  305.3 31.4 %all_to_all.22 = bf16[3,3,2,128,512]{4,3,1,0,2:T(8,128)(2,1)S(1)} all-to-all(bf16[3,3,2,128,512]{4,3,1,0,2:T(8,128)(2,1)} %rev.18), channel_id=1, replica_groups=mesh['lat'=4,'lon'=4,'mesh'=2] {'mesh'}, dimensions={2} | all-to-all | bytes 4718592 | tf_op jit(solution)/shard_map/all_to_all | solution.py:69
  338.6 16.0 %collective-permute-done.8 = bf16[1,3,2,128,512]{4,3,1,0,2:T(8,128)(2,1)S(1)} collective-permute-done((bf16[1,3,2,128,512]{4,3,1,0,2:T(8,128)(2,1)S(1)}, bf16[1,3,2,128,512]{4,3,1,0,2:T(8,128)(2,1)S(1)}, u32[]{:S(2)}, u32[]{:S(2)}) %collective-permute-start.8) | collective-permute-done | bytes 786464 | tf_op jit(solution)/shard_map/ppermute | solution.py:14
  363.6 29.9 %collective-permute-done.10 = bf16[5,1,2,128,512]{4,3,1,0,2:T(8,128)(2,1)S(1)} collective-permute-done((bf16[5,1,2,128,512]{4,3,1,0,2:T(8,128)(2,1)}, bf16[5,1,2,128,512]{4,3,1,0,2:T(8,128)(2,1)S(1)}, u32[]{:S(2)}, u32[]{:S(2)}) %collective-permute-start.10) | collective-permute-done | bytes 1310752 | tf_op jit(solution)/shard_map/ppermute | solution.py:14
  393.5 27.1 %collective-permute-done.11 = bf16[5,1,2,128,512]{4,3,1,0,2:T(8,128)(2,1)} collective-permute-done((bf16[5,1,2,128,512]{4,3,1,0,2:T(8,128)(2,1)}, bf16[5,1,2,128,512]{4,3,1,0,2:T(8,128)(2,1)}, u32[]{:S(2)}, u32[]{:S(2)}) %collective-permute-start.11) | collective-permute-done | bytes 1310752 | tf_op jit(solution)/shard_map/ppermute | solution.py:16
  427.5 16.6 %scatter_custom_fusion.2 = f32[320,512]{1,0:T(8,128)S(1)} fusion(s32[2304]{0:T(1024)S(1)} %reshape.251, f32[2304,512]{1,0:T(8,128)} %bitcast.57, f32[]{:T(128)} %constant.16.clone.1), kind=kCustom, calls=%fused_computation.63 | custom fusion | flops 1179648 | bytes 655872 | tf_op jit(solution)/shard_map/scatter-add | solution.py:148
  446.9 4.8 gather_fusion.3
  456.4 4.6 all-to-all-start.3
  461.8 19.0 %all-to-all-done.3 = bf16[3,3,2,85,512]{4,3,1,0,2:T(8,128)(2,1)} async-done(((bf16[3,3,2,85,512]{4,3,1,0,2:T(8,128)(2,1)}), bf16[3,3,2,85,512]{4,3,1,0,2:T(8,128)(2,1)}, u32[]{:S(2)}, u32[]{:S(2)}) %all-to-all-start.3) | async-done | bytes 1566752 | tf_op jit(solution)/shard_map/all_to_all | solution.py:62
  505.6 14.1 %collective-permute-done.15 = bf16[5,1,2,85,512]{4,2,3,1,0:T(2,128)(2,1)S(1)} collective-permute-done((bf16[5,1,2,85,512]{4,2,3,1,0:T(2,128)(2,1)S(1)}, bf16[5,1,2,85,512]{4,2,3,1,0:T(2,128)(2,1)S(1)}, u32[]{:S(2)}, u32[]{:S(2)}) %collective-permute-start.15) | collective-permute-done | bytes 870432 | tf_op jit(solution)/shard_map/ppermute | solution.py:16
  519.9 19.1 %collective-permute-done.14 = bf16[5,1,2,85,512]{4,2,3,1,0:T(2,128)(2,1)S(1)} collective-permute-done((bf16[5,1,2,85,512]{4,2,3,1,0:T(2,128)(2,1)S(1)}, bf16[5,1,2,85,512]{4,2,3,1,0:T(2,128)(2,1)S(1)}, u32[]{:S(2)}, u32[]{:S(2)}) %collective-permute-start.14) | collective-permute-done | bytes 870432 | tf_op jit(solution)/shard_map/ppermute | solution.py:14
  541.8 3.7 reshape.261
  545.5 11.6 %scatter_custom_fusion.3 = f32[1024,512]{1,0:T(8,128)} fusion(s32[1530]{0:T(1024)} %reshape.259, f32[1530,512]{1,0:T(8,128)} %reshape.261, f32[]{:T(128)} %constant.16.clone.1), kind=kCustom, calls=%fused_computation.44 | custom fusion | flops 783360 | bytes 2097664 | tf_op jit(solution)/shard_map/scatter-add | solution.py:160
  557.1 3.6 fusion.5
  561.7 3.7 convolution_add_fusion
  565.4 146.7 %all-reduce.3.cloned.1.call-done = (f32[512,512]{0,1:T(8,128)}, f32[512,512]{1,0:T(8,128)}, f32[512,512]{1,0:T(8,128)}, f32[512,512]{1,0:T(8,128)}, f32[512,512]{1,0:T(8,128)}, /*index=5*/f32[512,84]{1,0:T(8,128)}) async-done(((f32[512,512]{0,1:T(8,128)}, f32[512,512]{1,0:T(8,128)}, f32[512,512]{1,0:T(8,128)}, f32[512,512]{1,0:T(8,128)}, f32[512,512]{1,0:T(8,128)}, /*index=5*/f32[512,84]{1,0:T(8,128)}), ...) | async-done | bytes 5414928 | tf_op jit(solution)/shard_map/psum | solution.py:166
  (216 shorter events, 121.5 us)
Async XLA Ops:
  7.2 250.0 %copy-start = (bf16[512,512]{1,0:T(8,128)(2,1)S(1)}, bf16[512,512]{1,0:T(8,128)(2,1)}, u32[]{:S(2)}) copy-start(bf16[512,512]{1,0:T(8,128)(2,1)} %param.26) | copy-start | bytes 1572868
  46.6 11.7 %collective-permute-start = (bf16[1,3,2,85,512]{4,2,3,1,0:T(2,128)(2,1)S(1)}, bf16[1,3,2,85,512]{4,2,3,1,0:T(2,128)(2,1)S(1)}, u32[]{:S(2)}, u32[]{:S(2)}) collective-permute-start(bf16[1,3,2,85,512]{4,2,3,1,0:T(2,128)(2,1)S(1)} %copy.56), channel_id=1, source_target_pairs={{0,8},{8,16},{16,24},{24,0},{1,9},{9,17},{17,25},{25,1},{2,10},{10... | collective-permute-start | bytes 1566728 | tf_op jit(solution)/shard_map/ppermute | solution.py:14
  47.0 13.0 %collective-permute-start.1 = (bf16[1,3,2,85,512]{4,2,3,1,0:T(2,128)(2,1)S(1)}, bf16[1,3,2,85,512]{4,2,3,1,0:T(2,128)(2,1)S(1)}, u32[]{:S(2)}, u32[]{:S(2)}) collective-permute-start(bf16[1,3,2,85,512]{4,2,3,1,0:T(2,128)(2,1)S(1)} %copy.57), channel_id=1, source_target_pairs={{8,0},{16,8},{24,16},{0,24},{9,1},{17,9},{25,17},{1,25},{10,2},{18... | collective-permute-start | bytes 1566728 | tf_op jit(solution)/shard_map/ppermute | solution.py:16
  60.1 6.2 copy-start.10
  60.1 6.2 copy-start.35
  60.2 6.3 copy-start.27
  60.3 6.2 copy-start.37
  61.0 23.4 %collective-permute-start.3 = (bf16[5,1,2,85,512]{4,2,3,1,0:T(2,128)(2,1)S(1)}, bf16[5,1,2,85,512]{4,2,3,1,0:T(2,128)(2,1)S(1)}, u32[]{:S(2)}, u32[]{:S(2)}) collective-permute-start(bf16[5,1,2,85,512]{4,2,3,1,0:T(2,128)(2,1)S(1)} %copy.61), channel_id=1, source_target_pairs={{2,0},{4,2},{6,4},{0,6},{3,1},{5,3},{7,5},{1,7},{10,8},{12,10},{14... | collective-permute-start | bytes 2611208 | tf_op jit(solution)/shard_map/ppermute | solution.py:16
  66.3 37.6 %collective-permute-start.2 = (bf16[5,1,2,85,512]{4,2,3,1,0:T(2,128)(2,1)}, bf16[5,1,2,85,512]{4,2,3,1,0:T(2,128)(2,1)}, u32[]{:S(2)}, u32[]{:S(2)}) collective-permute-start(bf16[5,1,2,85,512]{4,2,3,1,0:T(2,128)(2,1)} %copy.60), channel_id=1, source_target_pairs={{0,2},{2,4},{4,6},{6,0},{1,3},{3,5},{5,7},{7,1},{8,10},{10,12},{12... | collective-permute-start | bytes 2611208 | tf_op jit(solution)/shard_map/ppermute | solution.py:14
  66.4 38.8 %copy-start.11 = (bf16[5,3,2,85,512]{4,3,1,0,2:T(8,128)(2,1)S(1)}, bf16[5,3,2,85,512]{4,3,1,0,2:T(8,128)(2,1)}, u32[]{:S(2)}) copy-start(bf16[5,3,2,85,512]{4,3,1,0,2:T(8,128)(2,1)} %copy-done.10) | copy-start | bytes 7833604
  112.0 11.4 %copy-start.17 = (bf16[512,512]{1,0:T(8,128)(2,1)S(1)}, bf16[512,512]{1,0:T(8,128)(2,1)}, u32[]{:S(2)}) copy-start(bf16[512,512]{1,0:T(8,128)(2,1)} %param.24) | copy-start | bytes 1572868
  112.0 11.4 %copy-start.38 = (f32[512]{0:T(512)S(1)}, f32[512]{0:T(512)}, u32[]{:S(2)}) copy-start(f32[512]{0:T(512)} %param.22) | copy-start | bytes 6148
  112.0 12.6 %copy-start.45 = (bf16[512,512]{1,0:T(8,128)(2,1)S(1)}, bf16[512,512]{1,0:T(8,128)(2,1)}, u32[]{:S(2)}) copy-start(bf16[512,512]{1,0:T(8,128)(2,1)} %param.25) | copy-start | bytes 1572868
  165.2 17.3 %collective-permute-start.4 = (bf16[1,3,2,128,512]{4,3,2,1,0:T(8,128)(2,1)S(1)}, bf16[1,3,2,128,512]{4,3,2,1,0:T(8,128)(2,1)S(1)}, u32[]{:S(2)}, u32[]{:S(2)}) collective-permute-start(bf16[1,3,2,128,512]{4,3,2,1,0:T(8,128)(2,1)S(1)} %copy.96), channel_id=1, source_target_pairs={{0,8},{8,16},{16,24},{24,0},{1,9},{9,17},{17,25},{25,1},{2,10},{10... | collective-permute-start | bytes 2359304 | tf_op jit(solution)/shard_map/ppermute | solution.py:14
  165.3 18.9 %collective-permute-start.5 = (bf16[1,3,2,128,512]{4,3,2,1,0:T(8,128)(2,1)S(1)}, bf16[1,3,2,128,512]{4,3,2,1,0:T(8,128)(2,1)S(1)}, u32[]{:S(2)}, u32[]{:S(2)}) collective-permute-start(bf16[1,3,2,128,512]{4,3,2,1,0:T(8,128)(2,1)S(1)} %copy.97), channel_id=1, source_target_pairs={{8,0},{16,8},{24,16},{0,24},{9,1},{17,9},{25,17},{1,25},{10,2},{18... | collective-permute-start | bytes 2359304 | tf_op jit(solution)/shard_map/ppermute | solution.py:16
  186.2 6.2 copy-start.42
  187.9 33.7 %collective-permute-start.6 = (bf16[5,1,2,128,512]{4,3,2,1,0:T(8,128)(2,1)}, bf16[5,1,2,128,512]{4,3,2,1,0:T(8,128)(2,1)S(1)}, u32[]{:S(2)}, u32[]{:S(2)}) collective-permute-start(bf16[5,1,2,128,512]{4,3,2,1,0:T(8,128)(2,1)} %get-tuple-element.43), channel_id=1, source_target_pairs={{0,2},{2,4},{4,6},{6,0},{1,3},{3,5},{5,7},{7,1},{8,10},{10,12},{12... | collective-permute-start | bytes 3932168 | tf_op jit(solution)/shard_map/ppermute | solution.py:14
  189.5 59.5 %collective-permute-start.7 = (bf16[5,1,2,128,512]{4,3,2,1,0:T(8,128)(2,1)}, bf16[5,1,2,128,512]{4,3,2,1,0:T(8,128)(2,1)}, u32[]{:S(2)}, u32[]{:S(2)}) collective-permute-start(bf16[5,1,2,128,512]{4,3,2,1,0:T(8,128)(2,1)} %get-tuple-element.44), channel_id=1, source_target_pairs={{2,0},{4,2},{6,4},{0,6},{3,1},{5,3},{7,5},{1,7},{10,8},{12,10},{14... | collective-permute-start | bytes 3932168 | tf_op jit(solution)/shard_map/ppermute | solution.py:16
  336.8 17.8 %collective-permute-start.8 = (bf16[1,3,2,128,512]{4,3,1,0,2:T(8,128)(2,1)S(1)}, bf16[1,3,2,128,512]{4,3,1,0,2:T(8,128)(2,1)S(1)}, u32[]{:S(2)}, u32[]{:S(2)}) collective-permute-start(bf16[1,3,2,128,512]{4,3,1,0,2:T(8,128)(2,1)S(1)} %get-tuple-element.50), channel_id=1, source_target_pairs={{0,8},{8,16},{16,24},{24,0},{1,9},{9,17},{17,25},{25,1},{2,10},{10... | collective-permute-start | bytes 2359304 | tf_op jit(solution)/shard_map/ppermute | solution.py:14
  336.9 19.2 %collective-permute-start.9 = (bf16[1,3,2,128,512]{4,3,1,0,2:T(8,128)(2,1)S(1)}, bf16[1,3,2,128,512]{4,3,1,0,2:T(8,128)(2,1)S(1)}, u32[]{:S(2)}, u32[]{:S(2)}) collective-permute-start(bf16[1,3,2,128,512]{4,3,1,0,2:T(8,128)(2,1)S(1)} %get-tuple-element.49), channel_id=1, source_target_pairs={{8,0},{16,8},{24,16},{0,24},{9,1},{17,9},{25,17},{1,25},{10,2},{18... | collective-permute-start | bytes 2359304 | tf_op jit(solution)/shard_map/ppermute | solution.py:16
  359.8 33.7 %collective-permute-start.10 = (bf16[5,1,2,128,512]{4,3,1,0,2:T(8,128)(2,1)}, bf16[5,1,2,128,512]{4,3,1,0,2:T(8,128)(2,1)S(1)}, u32[]{:S(2)}, u32[]{:S(2)}) collective-permute-start(bf16[5,1,2,128,512]{4,3,1,0,2:T(8,128)(2,1)} %get-tuple-element.41), channel_id=1, source_target_pairs={{0,2},{2,4},{4,6},{6,0},{1,3},{3,5},{5,7},{7,1},{8,10},{10,12},{12... | collective-permute-start | bytes 3932168 | tf_op jit(solution)/shard_map/ppermute | solution.py:14
  361.1 59.5 %collective-permute-start.11 = (bf16[5,1,2,128,512]{4,3,1,0,2:T(8,128)(2,1)}, bf16[5,1,2,128,512]{4,3,1,0,2:T(8,128)(2,1)}, u32[]{:S(2)}, u32[]{:S(2)}) collective-permute-start(bf16[5,1,2,128,512]{4,3,1,0,2:T(8,128)(2,1)} %get-tuple-element.42), channel_id=1, source_target_pairs={{2,0},{4,2},{6,4},{0,6},{3,1},{5,3},{7,5},{1,7},{10,8},{12,10},{14... | collective-permute-start | bytes 3932168 | tf_op jit(solution)/shard_map/ppermute | solution.py:16
  424.5 19.6 %copy-start.23 = (f32[320,512]{1,0:T(8,128)S(1)}, f32[320,512]{1,0:T(8,128)}, u32[]{:S(2)}) copy-start(f32[320,512]{1,0:T(8,128)} %copy-done.22) | copy-start | bytes 1966084
  427.5 18.4 %copy-start.18 = (bf16[512,512]{1,0:T(8,128)(2,1)S(1)}, bf16[512,512]{1,0:T(8,128)(2,1)}, u32[]{:S(2)}) copy-start(bf16[512,512]{1,0:T(8,128)(2,1)} %param.24) | copy-start | bytes 1572868
  427.5 18.4 %copy-start.39 = (f32[512]{0:T(512)S(1)}, f32[512]{0:T(512)}, u32[]{:S(2)}) copy-start(f32[512]{0:T(512)} %param.22) | copy-start | bytes 6148
  456.4 24.4 %all-to-all-start.3 = ((bf16[3,3,2,85,512]{4,3,1,0,2:T(8,128)(2,1)}), bf16[3,3,2,85,512]{4,3,1,0,2:T(8,128)(2,1)}, u32[]{:S(2)}, u32[]{:S(2)}) async-start(bf16[3,3,2,85,512]{4,3,1,0,2:T(8,128)(2,1)} %copy.71), calls=%async_computation.3 | async-start | bytes 3244032 | tf_op jit(solution)/shard_map/all_to_all | solution.py:62
  461.0 24.1 %copy-start.8 = (bf16[3,3,2,128,512]{4,3,2,1,0:T(8,128)(2,1)S(1)}, bf16[3,3,2,128,512]{4,3,2,1,0:T(8,128)(2,1)}, u32[]{:S(2)}) copy-start(bf16[3,3,2,128,512]{4,3,2,1,0:T(8,128)(2,1)} %copy-done.7) | copy-start | bytes 7077892
  461.1 251.0 %all-reduce.3.cloned.1.call-start = ((), (), s32[]{:S(2)}) async-start(), calls=%async_computation.4 | async-start | bytes 11010048 | tf_op jit(solution)/shard_map/psum | solution.py:166
  482.7 8.6 %collective-permute-start.12 = (bf16[1,3,2,85,512]{4,2,3,1,0:T(2,128)(2,1)S(1)}, bf16[1,3,2,85,512]{4,2,3,1,0:T(2,128)(2,1)S(1)}, u32[]{:S(2)}, u32[]{:S(2)}) collective-permute-start(bf16[1,3,2,85,512]{4,2,3,1,0:T(2,128)(2,1)S(1)} %copy.72), channel_id=1, source_target_pairs={{0,8},{8,16},{16,24},{24,0},{1,9},{9,17},{17,25},{25,1},{2,10},{10... | collective-permute-start | bytes 1566728 | tf_op jit(solution)/shard_map/ppermute | solution.py:14
  488.0 8.5 %collective-permute-start.13 = (bf16[1,3,2,85,512]{4,2,3,1,0:T(2,128)(2,1)S(1)}, bf16[1,3,2,85,512]{4,2,3,1,0:T(2,128)(2,1)S(1)}, u32[]{:S(2)}, u32[]{:S(2)}) collective-permute-start(bf16[1,3,2,85,512]{4,2,3,1,0:T(2,128)(2,1)S(1)} %copy.73), channel_id=1, source_target_pairs={{8,0},{16,8},{24,16},{0,24},{9,1},{17,9},{25,17},{1,25},{10,2},{18... | collective-permute-start | bytes 1566728 | tf_op jit(solution)/shard_map/ppermute | solution.py:16
  498.1 21.7 %collective-permute-start.15 = (bf16[5,1,2,85,512]{4,2,3,1,0:T(2,128)(2,1)S(1)}, bf16[5,1,2,85,512]{4,2,3,1,0:T(2,128)(2,1)S(1)}, u32[]{:S(2)}, u32[]{:S(2)}) collective-permute-start(bf16[5,1,2,85,512]{4,2,3,1,0:T(2,128)(2,1)S(1)} %copy.78), channel_id=1, source_target_pairs={{2,0},{4,2},{6,4},{0,6},{3,1},{5,3},{7,5},{1,7},{10,8},{12,10},{14... | collective-permute-start | bytes 2611208 | tf_op jit(solution)/shard_map/ppermute | solution.py:16
  500.5 38.5 %collective-permute-start.14 = (bf16[5,1,2,85,512]{4,2,3,1,0:T(2,128)(2,1)S(1)}, bf16[5,1,2,85,512]{4,2,3,1,0:T(2,128)(2,1)S(1)}, u32[]{:S(2)}, u32[]{:S(2)}) collective-permute-start(bf16[5,1,2,85,512]{4,2,3,1,0:T(2,128)(2,1)S(1)} %copy.77), channel_id=1, source_target_pairs={{0,2},{2,4},{4,6},{6,0},{1,3},{3,5},{5,7},{7,1},{8,10},{10,12},{12... | collective-permute-start | bytes 2611208 | tf_op jit(solution)/shard_map/ppermute | solution.py:14
  (32 other events, 95.2 us)
Sparse Core Ops, SparseCore 0:
  560.8 151.1 all-reduce.2
where the time goes:
time: 738 us; the launch traced here: 728 us
  waiting for transfers between devices  399 us (54%)
  local copies, waits for them, and re-layouts  88.6 us (12%)
  blocking collectives  85.8 us (12%)
  other arithmetic  81.7 us (11%)
  matrix products  31.4 us (4%)
  starting transfers between devices  26.5 us (4%)
  between operations  15.5 us (2%)
    psum x1, waiting for transfers between devices, on_device(): lax.psum((partials[0], partials[1], partials[2], partials[3], partials[4]...  147 us
    ppermute x8, waiting for transfers between devices, extended_2(): lax.ppermute(tail, axis, [(i, (i + 1) % count) for i in range(count)])  139 us
    ppermute x8, waiting for transfers between devices, extended_2(): lax.ppermute(head, axis, [((i + 1) % count, i) for i in range(count)])  93.7 us
    all_to_all x2, blocking collectives, route_dec(): lax.all_to_all(bucket, 'mesh', split_axis=2, concat_axis=2, tiled=True)  62 us
    all_to_all x1, blocking collectives, route_enc(): lax.all_to_all(bucket, 'mesh', split_axis=2, concat_axis=2, tiled=True)  23.8 us
    scatter-add x1, other arithmetic, on_device(): jax.ops.segment_sum(weighted, cell_ids, num_segments=cell_rows)  22 us
    all_to_all x1, waiting for transfers between devices, route_enc(): lax.all_to_all(bucket, 'mesh', split_axis=2, concat_axis=2, tiled=True)  19 us
    ppermute x8, starting transfers between devices, extended_2(): lax.ppermute(head, axis, [((i + 1) % count, i) for i in range(count)])  18.4 us
  transfers between devices with their start and end apart: 18, of which 18 were waited for; matrix products, arithmetic and copies ran while one was open for 3% of the time, Pallas kernels for 0%

commit v1 on v0

--- a/solution.py
+++ b/solution.py
@@ -1,7 +1,20 @@
+import functools
 import jax
 import jax.numpy as jnp
 from jax import lax
 from jax.sharding import PartitionSpec as P
+
+
+def _cut_vectors(body, across, dim_no, join_dim):
+    return jnp.concatenate(
+        lax.all_to_all(
+            jnp.stack(jnp.split(body, lax.axis_size(across), axis=dim_no)), across, 0, 0
+        ),
+        axis=join_dim,
+    )
+
+
+review_spans_for = functools.partial(_cut_vectors, across="mesh", dim_no=2, join_dim=2)
 
 
 def extended_2(cells, sides, width):
@@ -59,7 +72,7 @@
 
 
 def route_enc(bucket):
-    crossed = lax.all_to_all(bucket, "mesh", split_axis=2, concat_axis=2, tiled=True)
+    crossed = review_spans_for(bucket)
     extended = extended_2(crossed, (("lat", 0), ("lon", 1)), 1)
     result = extended[::-2, ::-2]
     return result

time: 738 us -> 736 us (level)
    ppermute x8, waiting for transfers between devices: 93.7 us -> 121 us  [extended_2(): lax.ppermute(head, axis, [((i + 1) % count, i) for i in range(count)])]
    ppermute x8, waiting for transfers between devices: 139 us -> 116 us  [extended_2(): lax.ppermute(tail, axis, [(i, (i + 1) % count) for i in range(count)])]
  transfers between devices with their start and end apart: 18 -> 18, of which waited for: 18 -> 15; matrix products, arithmetic and copies ran while one was open for 3% -> 3% of each run, Pallas kernels for 0% -> 0%
where the time goes in v1:
time: 736 us; the launch traced here: 726 us
  waiting for transfers between devices  403 us (55%)
  other arithmetic  85.7 us (12%)
  blocking collectives  84.4 us (11%)
  local copies, waits for them, and re-layouts  83.7 us (11%)
  matrix products  30.2 us (4%)
  starting transfers between devices  23.3 us (3%)
  between operations  15.5 us (2%)
    psum x1, waiting for transfers between devices, on_device(): lax.psum((partials[0], partials[1], partials[2], partials[3], partials[4]...  146 us
    ppermute x8, waiting for transfers between devices, extended_2(): lax.ppermute(head, axis, [((i + 1) % count, i) for i in range(count)])  121 us
    ppermute x8, waiting for transfers between devices, extended_2(): lax.ppermute(tail, axis, [(i, (i + 1) % count) for i in range(count)])  116 us
    all_to_all x2, blocking collectives, route_dec(): lax.all_to_all(bucket, 'mesh', split_axis=2, concat_axis=2, tiled=True)  60.6 us
    all_to_all x1, blocking collectives, _cut_vectors(): lax.all_to_all(jnp.stack(jnp.split(body, lax.axis_size(across), axis=dim_...  23.8 us
    scatter-add x1, other arithmetic, on_device(): jax.ops.segment_sum(weighted, cell_ids, num_segments=cell_rows)  22 us
    all_to_all x1, waiting for transfers between devices, _cut_vectors(): lax.all_to_all(jnp.stack(jnp.split(body, lax.axis_size(across), axis=dim_...  20 us
    dot_general x12, matrix products, matmul(): return jnp.dot(left, right, preferred_element_type=jnp.float32)  18.2 us
  transfers between devices with their start and end apart: 18, of which 15 were waited for; matrix products, arithmetic and copies ran while one was open for 3% of the time, Pallas kernels for 0%

profile of v1, /device:TPU:0, one launch (start us, length us, event | category | flops | bytes accessed | tf_op | source)
XLA Modules:
  0.0 725.6 jit_solution(3667351885721585002)
XLA Ops:
  12.3 4.8 gather_fusion
  22.4 23.8 %all_to_all.20 = bf16[2,3,3,1,85,512]{5,4,2,1,3,0:T(8,128)(2,1)S(1)} all-to-all(bf16[2,3,3,1,85,512]{5,4,2,1,3,0:T(8,128)(2,1)S(1)} %pad_maximum_fusion.4), channel_id=1, replica_groups=mesh['lat'=4,'lon'=4,'mesh'=2] {'mesh'}, dimensions={0} | all-to-all | bytes 3133440 | tf_op jit(solution)/shard_map/all_to_all | solution.py:10
  47.7 10.2 %collective-permute-done.1 = bf16[1,3,2,85,512]{4,2,3,1,0:T(2,128)(2,1)S(1)} collective-permute-done((bf16[1,3,2,85,512]{4,2,3,1,0:T(2,128)(2,1)S(1)}, bf16[1,3,2,85,512]{4,2,3,1,0:T(2,128)(2,1)S(1)}, u32[]{:S(2)}, u32[]{:S(2)}) %collective-permute-start.1) | collective-permute-done | bytes 522272 | tf_op jit(solution)/shard_map/ppermute | solution.py:29
  63.1 3.6 collective-permute-start.3
  70.2 16.6 %collective-permute-done.3 = bf16[5,1,2,85,512]{4,2,3,1,0:T(2,128)(2,1)} collective-permute-done((bf16[5,1,2,85,512]{4,2,3,1,0:T(2,128)(2,1)}, bf16[5,1,2,85,512]{4,2,3,1,0:T(2,128)(2,1)}, u32[]{:S(2)}, u32[]{:S(2)}) %collective-permute-start.3) | collective-permute-done | bytes 870432 | tf_op jit(solution)/shard_map/ppermute | solution.py:29
  88.1 17.0 %collective-permute-done.2 = bf16[5,1,2,85,512]{4,2,3,1,0:T(2,128)(2,1)} collective-permute-done((bf16[5,1,2,85,512]{4,2,3,1,0:T(2,128)(2,1)}, bf16[5,1,2,85,512]{4,2,3,1,0:T(2,128)(2,1)}, u32[]{:S(2)}, u32[]{:S(2)}) %collective-permute-start.2) | collective-permute-done | bytes 870432 | tf_op jit(solution)/shard_map/ppermute | solution.py:27
  110.7 3.7 reshape.257
  114.4 10.5 %scatter_fusion = f32[320,512]{1,0:T(8,128)S(1)} fusion(f32[320,512]{1,0:T(8,128)S(1)} %convert_element_type.79, s32[1530]{0:T(1024)S(1)} %reshape.255, f32[1530,512]{1,0:T(8,128)} %reshape.257), kind=kCustom, calls=%fused_computation.4 | custom fusion | flops 783360 | bytes 9406440 | tf_op jit(solution)/shard_map/scatter-add | solution.py:131
  127.3 7.5 %gather_fusion.1 = bf16[2304,512]{1,0:T(8,128)(2,1)} fusion(bf16[320,512]{1,0:T(8,128)(2,1)S(1)} %fusion.6, s32[3072]{0:T(1024)S(1)} %get-tuple-element.68), kind=kCustom, calls=%fused_computation.1 | custom fusion | bytes 4727808 | tf_op jit(solution)/shard_map/gather | solution.py:139
  136.6 29.6 %all_to_all.21 = bf16[3,3,2,128,512]{4,3,1,0,2:T(8,128)(2,1)S(1)} all-to-all(bf16[3,3,2,128,512]{4,3,1,0,2:T(8,128)(2,1)S(1)} %copy.79), channel_id=1, replica_groups=mesh['lat'=4,'lon'=4,'mesh'=2] {'mesh'}, dimensions={2} | all-to-all | bytes 4718592 | tf_op jit(solution)/shard_map/all_to_all | solution.py:82
  168.9 17.7 %collective-permute-done.4 = bf16[1,3,2,128,512]{4,3,2,1,0:T(8,128)(2,1)S(1)} collective-permute-done((bf16[1,3,2,128,512]{4,3,2,1,0:T(8,128)(2,1)S(1)}, bf16[1,3,2,128,512]{4,3,2,1,0:T(8,128)(2,1)S(1)}, u32[]{:S(2)}, u32[]{:S(2)}) %collective-permute-start.4) | collective-permute-done | bytes 786464 | tf_op jit(solution)/shard_map/ppermute | solution.py:27
  194.7 29.1 %collective-permute-done.6 = bf16[5,1,2,128,512]{4,3,2,1,0:T(8,128)(2,1)S(1)} collective-permute-done((bf16[5,1,2,128,512]{4,3,2,1,0:T(8,128)(2,1)}, bf16[5,1,2,128,512]{4,3,2,1,0:T(8,128)(2,1)S(1)}, u32[]{:S(2)}, u32[]{:S(2)}) %collective-permute-start.6) | collective-permute-done | bytes 1310752 | tf_op jit(solution)/shard_map/ppermute | solution.py:27
  223.8 26.5 %collective-permute-done.7 = bf16[5,1,2,128,512]{4,3,2,1,0:T(8,128)(2,1)} collective-permute-done((bf16[5,1,2,128,512]{4,3,2,1,0:T(8,128)(2,1)}, bf16[5,1,2,128,512]{4,3,2,1,0:T(8,128)(2,1)}, u32[]{:S(2)}, u32[]{:S(2)}) %collective-permute-start.7) | collective-permute-done | bytes 1310752 | tf_op jit(solution)/shard_map/ppermute | solution.py:29
  258.6 3.6 fusion.30
  262.2 22.0 %scatter_custom_fusion.1 = f32[1024,512]{1,0:T(8,128)S(1)} fusion(s32[2304]{0:T(1024)} %reshape.263, f32[2304,512]{1,0:T(8,128)} %fusion.30, f32[]{:T(128)} %constant.24.clone.1, f32[2304]{0:T(1024)S(1)} %broadcast_select_fusion, f32[]{:T(128)} %constant.16.clone.1), kind=kCustom, calls=%fused_computation.11 | custom fusion | flops 7077888 | bytes 6825984 | tf_op jit(solution)/shard_map/scatter-add | solution.py:146
  291.8 7.6 %gather_fusion.2 = bf16[2304,512]{1,0:T(8,128)(2,1)} fusion(bf16[1024,512]{1,0:T(8,128)(2,1)S(1)} %convolution_convert_fusion.1, s32[3072]{0:T(1024)S(1)} %copy-done.31), kind=kCustom, calls=%fused_computation.2 | custom fusion | bytes 4727808 | tf_op jit(solution)/shard_map/gather | solution.py:156
  299.3 4.1 multiply_convert_fusion
  306.7 31.1 %all_to_all.22 = bf16[3,3,2,128,512]{4,3,1,0,2:T(8,128)(2,1)S(1)} all-to-all(bf16[3,3,2,128,512]{4,3,1,0,2:T(8,128)(2,1)} %rev.16), channel_id=1, replica_groups=mesh['lat'=4,'lon'=4,'mesh'=2] {'mesh'}, dimensions={2} | all-to-all | bytes 4718592 | tf_op jit(solution)/shard_map/all_to_all | solution.py:82
  339.7 17.8 %collective-permute-done.8 = bf16[1,3,2,128,512]{4,3,1,0,2:T(8,128)(2,1)S(1)} collective-permute-done((bf16[1,3,2,128,512]{4,3,1,0,2:T(8,128)(2,1)S(1)}, bf16[1,3,2,128,512]{4,3,1,0,2:T(8,128)(2,1)S(1)}, u32[]{:S(2)}, u32[]{:S(2)}) %collective-permute-start.8) | collective-permute-done | bytes 786464 | tf_op jit(solution)/shard_map/ppermute | solution.py:27
  364.4 29.9 %collective-permute-done.10 = bf16[5,1,2,128,512]{4,3,1,0,2:T(8,128)(2,1)S(1)} collective-permute-done((bf16[5,1,2,128,512]{4,3,1,0,2:T(8,128)(2,1)}, bf16[5,1,2,128,512]{4,3,1,0,2:T(8,128)(2,1)S(1)}, u32[]{:S(2)}, u32[]{:S(2)}) %collective-permute-start.10) | collective-permute-done | bytes 1310752 | tf_op jit(solution)/shard_map/ppermute | solution.py:27
  394.3 27.1 %collective-permute-done.11 = bf16[5,1,2,128,512]{4,3,1,0,2:T(8,128)(2,1)} collective-permute-done((bf16[5,1,2,128,512]{4,3,1,0,2:T(8,128)(2,1)}, bf16[5,1,2,128,512]{4,3,1,0,2:T(8,128)(2,1)}, u32[]{:S(2)}, u32[]{:S(2)}) %collective-permute-start.11) | collective-permute-done | bytes 1310752 | tf_op jit(solution)/shard_map/ppermute | solution.py:29
  428.3 16.6 %scatter_custom_fusion.2 = f32[320,512]{1,0:T(8,128)S(1)} fusion(s32[2304]{0:T(1024)S(1)} %reshape.271, f32[2304,512]{1,0:T(8,128)} %bitcast.94, f32[]{:T(128)} %constant.16.clone.1), kind=kCustom, calls=%fused_computation.77 | custom fusion | flops 1179648 | bytes 655872 | tf_op jit(solution)/shard_map/scatter-add | solution.py:161
  447.7 4.8 gather_fusion.3
  457.3 3.8 all-to-all-start.3
  461.2 20.0 %all-to-all-done.3 = bf16[2,3,3,1,85,512]{5,4,2,3,1,0:T(8,128)(2,1)S(1)} async-done(((bf16[2,3,3,1,85,512]{5,4,2,3,1,0:T(8,128)(2,1)}), bf16[2,3,3,1,85,512]{5,4,2,3,1,0:T(8,128)(2,1)S(1)}, u32[]{:S(2)}, u32[]{:S(2)}) %all-to-all-start.3) | async-done | bytes 1566752 | tf_op jit(solution)/shard_map/all_to_all | solution.py:10
  486.6 8.0 %collective-permute-done.13 = bf16[1,3,2,85,512]{4,2,3,1,0:T(2,128)(2,1)S(1)} collective-permute-done((bf16[1,3,2,85,512]{4,2,3,1,0:T(2,128)(2,1)S(1)}, bf16[1,3,2,85,512]{4,2,3,1,0:T(2,128)(2,1)S(1)}, u32[]{:S(2)}, u32[]{:S(2)}) %collective-permute-start.13) | collective-permute-done | bytes 522272 | tf_op jit(solution)/shard_map/ppermute | solution.py:29
  504.8 32.3 %collective-permute-done.15 = bf16[5,1,2,85,512]{4,2,3,1,0:T(2,128)(2,1)S(1)} collective-permute-done((bf16[5,1,2,85,512]{4,2,3,1,0:T(2,128)(2,1)S(1)}, bf16[5,1,2,85,512]{4,2,3,1,0:T(2,128)(2,1)S(1)}, u32[]{:S(2)}, u32[]{:S(2)}) %collective-permute-start.15) | collective-permute-done | bytes 870432 | tf_op jit(solution)/shard_map/ppermute | solution.py:29
  540.2 3.7 reshape.281
  543.8 11.6 %scatter_custom_fusion.3 = f32[1024,512]{1,0:T(8,128)} fusion(s32[1530]{0:T(1024)S(1)} %reshape.279, f32[1530,512]{1,0:T(8,128)} %reshape.281, f32[]{:T(128)} %constant.16.clone.1), kind=kCustom, calls=%fused_computation.47 | custom fusion | flops 783360 | bytes 2097664 | tf_op jit(solution)/shard_map/scatter-add | solution.py:173
  555.5 3.6 fusion.5
  560.1 3.7 convolution_add_fusion
  563.7 146.0 %all-reduce.3.cloned.1.call-done = (f32[512,512]{0,1:T(8,128)}, f32[512,512]{1,0:T(8,128)}, f32[512,512]{1,0:T(8,128)}, f32[512,512]{1,0:T(8,128)}, f32[512,512]{1,0:T(8,128)}, /*index=5*/f32[512,84]{1,0:T(8,128)}) async-done(((f32[512,512]{0,1:T(8,128)}, f32[512,512]{1,0:T(8,128)}, f32[512,512]{1,0:T(8,128)}, f32[512,512]{1,0:T(8,128)}, f32[512,512]{1,0:T(8,128)}, /*index=5*/f32[512,84]{1,0:T(8,128)}), ...) | async-done | bytes 5414928 | tf_op jit(solution)/shard_map/psum | solution.py:179
  (216 shorter events, 112.5 us)
Async XLA Ops:
  7.2 251.4 %copy-start = (bf16[512,512]{1,0:T(8,128)(2,1)S(1)}, bf16[512,512]{1,0:T(8,128)(2,1)}, u32[]{:S(2)}) copy-start(bf16[512,512]{1,0:T(8,128)(2,1)} %param.26) | copy-start | bytes 1572868
  46.7 11.2 %collective-permute-start.1 = (bf16[1,3,2,85,512]{4,2,3,1,0:T(2,128)(2,1)S(1)}, bf16[1,3,2,85,512]{4,2,3,1,0:T(2,128)(2,1)S(1)}, u32[]{:S(2)}, u32[]{:S(2)}) collective-permute-start(bf16[1,3,2,85,512]{4,2,3,1,0:T(2,128)(2,1)S(1)} %copy.71), channel_id=1, source_target_pairs={{8,0},{16,8},{24,16},{0,24},{9,1},{17,9},{25,17},{1,25},{10,2},{18... | collective-permute-start | bytes 1566728 | tf_op jit(solution)/shard_map/ppermute | solution.py:29
  47.4 13.8 %collective-permute-start = (bf16[1,3,2,85,512]{4,2,3,1,0:T(2,128)(2,1)S(1)}, bf16[1,3,2,85,512]{4,2,3,1,0:T(2,128)(2,1)S(1)}, u32[]{:S(2)}, u32[]{:S(2)}) collective-permute-start(bf16[1,3,2,85,512]{4,2,3,1,0:T(2,128)(2,1)S(1)} %copy.70), channel_id=1, source_target_pairs={{0,8},{8,16},{16,24},{24,0},{1,9},{9,17},{17,25},{25,1},{2,10},{10... | collective-permute-start | bytes 1566728 | tf_op jit(solution)/shard_map/ppermute | solution.py:27
  61.5 6.8 copy-start.33
  61.5 6.9 copy-start.35
  61.6 8.0 %copy-start.37 = (s32[1,3,3,2,128]{4,3,2,1,0:T(2,128)S(1)}, s32[1,3,3,2,128]{4,3,2,1,0:T(2,128)}, u32[]{:S(2)}) copy-start(s32[1,3,3,2,128]{4,3,2,1,0:T(2,128)} %param.34) | copy-start | bytes 27652
  63.1 23.7 %collective-permute-start.3 = (bf16[5,1,2,85,512]{4,2,3,1,0:T(2,128)(2,1)}, bf16[5,1,2,85,512]{4,2,3,1,0:T(2,128)(2,1)}, u32[]{:S(2)}, u32[]{:S(2)}) collective-permute-start(bf16[5,1,2,85,512]{4,2,3,1,0:T(2,128)(2,1)} %copy.75), channel_id=1, source_target_pairs={{2,0},{4,2},{6,4},{0,6},{3,1},{5,3},{7,5},{1,7},{10,8},{12,10},{14... | collective-permute-start | bytes 2611208 | tf_op jit(solution)/shard_map/ppermute | solution.py:29
  68.3 36.8 %collective-permute-start.2 = (bf16[5,1,2,85,512]{4,2,3,1,0:T(2,128)(2,1)}, bf16[5,1,2,85,512]{4,2,3,1,0:T(2,128)(2,1)}, u32[]{:S(2)}, u32[]{:S(2)}) collective-permute-start(bf16[5,1,2,85,512]{4,2,3,1,0:T(2,128)(2,1)} %copy.74), channel_id=1, source_target_pairs={{0,2},{2,4},{4,6},{6,0},{1,3},{3,5},{5,7},{7,1},{8,10},{10,12},{12... | collective-permute-start | bytes 2611208 | tf_op jit(solution)/shard_map/ppermute | solution.py:27
  114.4 11.3 %copy-start.17 = (bf16[512,512]{1,0:T(8,128)(2,1)S(1)}, bf16[512,512]{1,0:T(8,128)(2,1)}, u32[]{:S(2)}) copy-start(bf16[512,512]{1,0:T(8,128)(2,1)} %param.24) | copy-start | bytes 1572868
  114.4 11.3 %copy-start.38 = (f32[512]{0:T(512)S(1)}, f32[512]{0:T(512)}, u32[]{:S(2)}) copy-start(f32[512]{0:T(512)} %param.22) | copy-start | bytes 6148
  166.4 20.1 %collective-permute-start.4 = (bf16[1,3,2,128,512]{4,3,2,1,0:T(8,128)(2,1)S(1)}, bf16[1,3,2,128,512]{4,3,2,1,0:T(8,128)(2,1)S(1)}, u32[]{:S(2)}, u32[]{:S(2)}) collective-permute-start(bf16[1,3,2,128,512]{4,3,2,1,0:T(8,128)(2,1)S(1)} %copy.110), channel_id=1, source_target_pairs={{0,8},{8,16},{16,24},{24,0},{1,9},{9,17},{17,25},{25,1},{2,10},{10... | collective-permute-start | bytes 2359304 | tf_op jit(solution)/shard_map/ppermute | solution.py:27
  167.1 19.7 %collective-permute-start.5 = (bf16[1,3,2,128,512]{4,3,2,1,0:T(8,128)(2,1)S(1)}, bf16[1,3,2,128,512]{4,3,2,1,0:T(8,128)(2,1)S(1)}, u32[]{:S(2)}, u32[]{:S(2)}) collective-permute-start(bf16[1,3,2,128,512]{4,3,2,1,0:T(8,128)(2,1)S(1)} %copy.111), channel_id=1, source_target_pairs={{8,0},{16,8},{24,16},{0,24},{9,1},{17,9},{25,17},{1,25},{10,2},{18... | collective-permute-start | bytes 2359304 | tf_op jit(solution)/shard_map/ppermute | solution.py:29
  186.9 7.8 %copy-start.41 = (f32[1,3,3,2,128]{4,3,2,1,0:T(2,128)S(1)}, f32[1,3,3,2,128]{4,3,2,1,0:T(2,128)}, u32[]{:S(2)}) copy-start(f32[1,3,3,2,128]{4,3,2,1,0:T(2,128)} %param.35) | copy-start | bytes 27652
  189.6 34.2 %collective-permute-start.6 = (bf16[5,1,2,128,512]{4,3,2,1,0:T(8,128)(2,1)}, bf16[5,1,2,128,512]{4,3,2,1,0:T(8,128)(2,1)S(1)}, u32[]{:S(2)}, u32[]{:S(2)}) collective-permute-start(bf16[5,1,2,128,512]{4,3,2,1,0:T(8,128)(2,1)} %get-tuple-element.43), channel_id=1, source_target_pairs={{0,2},{2,4},{4,6},{6,0},{1,3},{3,5},{5,7},{7,1},{8,10},{10,12},{12... | collective-permute-start | bytes 3932168 | tf_op jit(solution)/shard_map/ppermute | solution.py:27
  191.5 58.8 %collective-permute-start.7 = (bf16[5,1,2,128,512]{4,3,2,1,0:T(8,128)(2,1)}, bf16[5,1,2,128,512]{4,3,2,1,0:T(8,128)(2,1)}, u32[]{:S(2)}, u32[]{:S(2)}) collective-permute-start(bf16[5,1,2,128,512]{4,3,2,1,0:T(8,128)(2,1)} %get-tuple-element.44), channel_id=1, source_target_pairs={{2,0},{4,2},{6,4},{0,6},{3,1},{5,3},{7,5},{1,7},{10,8},{12,10},{14... | collective-permute-start | bytes 3932168 | tf_op jit(solution)/shard_map/ppermute | solution.py:29
  337.9 19.6 %collective-permute-start.8 = (bf16[1,3,2,128,512]{4,3,1,0,2:T(8,128)(2,1)S(1)}, bf16[1,3,2,128,512]{4,3,1,0,2:T(8,128)(2,1)S(1)}, u32[]{:S(2)}, u32[]{:S(2)}) collective-permute-start(bf16[1,3,2,128,512]{4,3,1,0,2:T(8,128)(2,1)S(1)} %get-tuple-element.50), channel_id=1, source_target_pairs={{0,8},{8,16},{16,24},{24,0},{1,9},{9,17},{17,25},{25,1},{2,10},{10... | collective-permute-start | bytes 2359304 | tf_op jit(solution)/shard_map/ppermute | solution.py:27
  337.9 19.8 %collective-permute-start.9 = (bf16[1,3,2,128,512]{4,3,1,0,2:T(8,128)(2,1)S(1)}, bf16[1,3,2,128,512]{4,3,1,0,2:T(8,128)(2,1)S(1)}, u32[]{:S(2)}, u32[]{:S(2)}) collective-permute-start(bf16[1,3,2,128,512]{4,3,1,0,2:T(8,128)(2,1)S(1)} %get-tuple-element.49), channel_id=1, source_target_pairs={{8,0},{16,8},{24,16},{0,24},{9,1},{17,9},{25,17},{1,25},{10,2},{18... | collective-permute-start | bytes 2359304 | tf_op jit(solution)/shard_map/ppermute | solution.py:29
  357.8 6.6 copy-start.36
  360.6 33.7 %collective-permute-start.10 = (bf16[5,1,2,128,512]{4,3,1,0,2:T(8,128)(2,1)}, bf16[5,1,2,128,512]{4,3,1,0,2:T(8,128)(2,1)S(1)}, u32[]{:S(2)}, u32[]{:S(2)}) collective-permute-start(bf16[5,1,2,128,512]{4,3,1,0,2:T(8,128)(2,1)} %get-tuple-element.41), channel_id=1, source_target_pairs={{0,2},{2,4},{4,6},{6,0},{1,3},{3,5},{5,7},{7,1},{8,10},{10,12},{12... | collective-permute-start | bytes 3932168 | tf_op jit(solution)/shard_map/ppermute | solution.py:27
  362.9 58.5 %collective-permute-start.11 = (bf16[5,1,2,128,512]{4,3,1,0,2:T(8,128)(2,1)}, bf16[5,1,2,128,512]{4,3,1,0,2:T(8,128)(2,1)}, u32[]{:S(2)}, u32[]{:S(2)}) collective-permute-start(bf16[5,1,2,128,512]{4,3,1,0,2:T(8,128)(2,1)} %get-tuple-element.42), channel_id=1, source_target_pairs={{2,0},{4,2},{6,4},{0,6},{3,1},{5,3},{7,5},{1,7},{10,8},{12,10},{14... | collective-permute-start | bytes 3932168 | tf_op jit(solution)/shard_map/ppermute | solution.py:29
  425.3 19.6 %copy-start.24 = (f32[320,512]{1,0:T(8,128)S(1)}, f32[320,512]{1,0:T(8,128)}, u32[]{:S(2)}) copy-start(f32[320,512]{1,0:T(8,128)} %copy-done.23) | copy-start | bytes 1966084
  428.3 18.4 %copy-start.18 = (bf16[512,512]{1,0:T(8,128)(2,1)S(1)}, bf16[512,512]{1,0:T(8,128)(2,1)}, u32[]{:S(2)}) copy-start(bf16[512,512]{1,0:T(8,128)(2,1)} %param.24) | copy-start | bytes 1572868
  428.3 18.4 %copy-start.39 = (f32[512]{0:T(512)S(1)}, f32[512]{0:T(512)}, u32[]{:S(2)}) copy-start(f32[512]{0:T(512)} %param.22) | copy-start | bytes 6148
  457.3 24.0 %all-to-all-start.3 = ((bf16[2,3,3,1,85,512]{5,4,2,3,1,0:T(8,128)(2,1)}), bf16[2,3,3,1,85,512]{5,4,2,3,1,0:T(8,128)(2,1)S(1)}, u32[]{:S(2)}, u32[]{:S(2)}) async-start(bf16[2,3,3,1,85,512]{5,4,2,3,1,0:T(8,128)(2,1)} %maximum_bitcast_fusion), calls=%async_computation.3 | async-start | bytes 3244032 | tf_op jit(solution)/shard_map/all_to_all | solution.py:10
  461.1 248.7 %all-reduce.3.cloned.1.call-start = ((), (), s32[]{:S(2)}) async-start(), calls=%async_computation.4 | async-start | bytes 11010048 | tf_op jit(solution)/shard_map/psum | solution.py:179
  482.4 12.1 %collective-permute-start.13 = (bf16[1,3,2,85,512]{4,2,3,1,0:T(2,128)(2,1)S(1)}, bf16[1,3,2,85,512]{4,2,3,1,0:T(2,128)(2,1)S(1)}, u32[]{:S(2)}, u32[]{:S(2)}) collective-permute-start(bf16[1,3,2,85,512]{4,2,3,1,0:T(2,128)(2,1)S(1)} %copy.89), channel_id=1, source_target_pairs={{8,0},{16,8},{24,16},{0,24},{9,1},{17,9},{25,17},{1,25},{10,2},{18... | collective-permute-start | bytes 1566728 | tf_op jit(solution)/shard_map/ppermute | solution.py:29
  482.5 13.5 %collective-permute-start.12 = (bf16[1,3,2,85,512]{4,2,3,1,0:T(2,128)(2,1)S(1)}, bf16[1,3,2,85,512]{4,2,3,1,0:T(2,128)(2,1)S(1)}, u32[]{:S(2)}, u32[]{:S(2)}) collective-permute-start(bf16[1,3,2,85,512]{4,2,3,1,0:T(2,128)(2,1)S(1)} %copy.88), channel_id=1, source_target_pairs={{0,8},{8,16},{16,24},{24,0},{1,9},{9,17},{17,25},{25,1},{2,10},{10... | collective-permute-start | bytes 1566728 | tf_op jit(solution)/shard_map/ppermute | solution.py:27
  497.6 4.2 copy-start.22
  497.7 5.7 copy-start.13
  497.7 5.7 copy-start.25
  497.7 39.4 %collective-permute-start.15 = (bf16[5,1,2,85,512]{4,2,3,1,0:T(2,128)(2,1)S(1)}, bf16[5,1,2,85,512]{4,2,3,1,0:T(2,128)(2,1)S(1)}, u32[]{:S(2)}, u32[]{:S(2)}) collective-permute-start(bf16[5,1,2,85,512]{4,2,3,1,0:T(2,128)(2,1)S(1)} %copy.93), channel_id=1, source_target_pairs={{2,0},{4,2},{6,4},{0,6},{3,1},{5,3},{7,5},{1,7},{10,8},{12,10},{14... | collective-permute-start | bytes 2611208 | tf_op jit(solution)/shard_map/ppermute | solution.py:29
  498.3 38.9 %collective-permute-start.14 = (bf16[5,1,2,85,512]{4,2,3,1,0:T(2,128)(2,1)S(1)}, bf16[5,1,2,85,512]{4,2,3,1,0:T(2,128)(2,1)S(1)}, u32[]{:S(2)}, u32[]{:S(2)}) collective-permute-start(bf16[5,1,2,85,512]{4,2,3,1,0:T(2,128)(2,1)S(1)} %copy.92), channel_id=1, source_target_pairs={{0,2},{2,4},{4,6},{6,0},{1,3},{3,5},{5,7},{7,1},{8,10},{10,12},{12... | collective-permute-start | bytes 2611208 | tf_op jit(solution)/shard_map/ppermute | solution.py:27
  (31 other events, 65.9 us)
Sparse Core Ops, SparseCore 0:
  559.2 150.5 all-reduce.2
